TPU v7x, 32 devices: a whole 2x2x4 slice. The times are simulated.
32 devices in a mesh: pipe: 4 (over y, x), row: 4 (over z), col: 2 (over core).
Axes of the slice: x: 2, y: 2, z: 4, core: 2. Of those that a mesh axis runs over, the one named last changes fastest.
Arguments:
- acts: bfloat16 [4, 1, 1024, 4, 128], P('pipe', None, 'col', 'row'), may hold values from -6 to 6
- weights: bfloat16 [4, 27, 1024, 1024], P('pipe', None, 'row', 'col'), may hold values from -0.0390625 to 0.0390625
- grad_top: bfloat16 [1, 1024, 4, 128], P(None, 'col', 'row'), may hold values from -6 to 6
Outputs:
- section_grads: bfloat16 [4, 1, 1024, 4, 128], P('pipe', None, 'col', 'row')
- weight_grads: bfloat16 [4, 27, 1024, 1024], P('pipe', None, 'row', 'col')
All inputs are finite; a program needn't handle non-finite values.
Results may differ from a plain program's by a relative error of at most 0.02.
Values may be sent and summed in bfloat16 or wider, within the bound.
A program may use at most 128 MiB of HBM per device.

v0:
```python
import functools
import math

import jax
import jax.numpy as jnp
from jax import lax
from jax.experimental import pallas as pl
from jax.experimental.pallas import tpu as pltpu
from jax.sharding import PartitionSpec as P

SZ = 16
MESH = pl.DeviceIdType.MESH


def moved_rows(block, shift):
    if shift == 0:
        return block
    wide = block.astype(jnp.float32)
    rows = wide.shape[0]
    rolled = pltpu.roll(wide, shift % rows, axis=0)
    column = lax.broadcasted_iota(jnp.int32, wide.shape, 0) % SZ
    inside = (column - shift >= 0) & (column - shift < SZ)
    return jnp.where(inside, rolled, jnp.zeros_like(rolled)).astype(block.dtype)


def chain_kernel(
    sections, rows, cols, per_col,
    w_hbm, act_ref, top_ref,
    sg_out, gin_out, act_out,
    w_vmem, gin, gbuf, acc, sbuf, pbuf, gout, act_all, sg,
    w_sem, top_send, gin_recv, fwd_send, act_send, act_recv,
    part_send, part_recv, pipe_send, out_send, out_recv,
):
    s, r, c = lax.axis_index("pipe"), lax.axis_index("row"), lax.axis_index("col")
    home = r // per_col
    slot = r % per_col
    cells, width = act_ref.shape[1], act_ref.shape[2]
    is_home = c == home
    is_top = s == sections - 1

    def remote(src, dst, send, recv, **where):
        return pltpu.make_async_remote_copy(
            src_ref=src, dst_ref=dst, send_sem=send, recv_sem=recv,
            device_id=where, device_id_type=MESH,
        )

    w_copy = pltpu.make_async_copy(w_hbm, w_vmem, w_sem)
    w_copy.start()

    barrier = pltpu.get_barrier_semaphore()
    for step in range(1, rows * cols):
        other = lax.rem(r * cols + c + step, rows * cols)
        pl.semaphore_signal(
            barrier, inc=1, device_id={"row": other // cols, "col": other % cols},
            device_id_type=MESH,
        )
    for step in (1, sections - 1):
        pl.semaphore_signal(
            barrier, inc=1, device_id={"pipe": lax.rem(s + step, sections)},
            device_id_type=MESH,
        )
    gbuf[...] = jnp.zeros_like(gbuf)
    pl.semaphore_wait(barrier, rows * cols + 1)

    def top_copy(j, q):
        return remote(
            top_ref.at[j], gin.at[r], top_send.at[j * cols + q], gin_recv.at[r],
            row=c * per_col + j, col=q,
        )

    def top_is_far(j, q):
        return is_top & ~((c * per_col + j == r) & (q == c))

    for j in range(per_col):
        for q in range(cols):
            @pl.when(top_is_far(j, q))
            def _():
                top_copy(j, q).start()

    @pl.when(is_top & is_home)
    def _():
        gin[r] = top_ref[slot]

    def act_copy(row):
        return remote(act_ref, act_all.at[r], act_send.at[row], act_recv.at[r], row=row)

    for row in range(rows):
        @pl.when(row != r)
        def _():
            act_copy(row).start()
    act_all[r] = act_ref[...]

    def fwd_copy(p, q):
        return remote(gin.at[p], gin.at[p], fwd_send.at[p, q], gin_recv.at[p], col=q)

    forwards = is_home & (s < sections - 1)
    for p in range(rows):
        @pl.when(~(is_top & is_home & (p == r)))
        def _():
            remote(gin.at[p], gin.at[p], fwd_send.at[p, 0], gin_recv.at[p], col=c).wait_recv()
        for q in range(cols):
            @pl.when(forwards & (q != c))
            def _():
                fwd_copy(p, q).start()
        for k in range(3):
            gbuf[p + 1, SZ:SZ + cells, k * width:(k + 1) * width] = moved_rows(gin[p], k - 1)

    w_copy.wait()

    def part_copy(j):
        return remote(
            sbuf.at[j], pbuf.at[r], part_send.at[j], part_recv.at[r], row=c * per_col + j,
        )

    for j in range(per_col):
        acc[...] = jnp.zeros_like(acc)

        def tap_plane(t, carry):
            start = pl.multiple_of((2 - t % 3) * SZ, SZ)
            left = gbuf[pl.ds(2 - t // 3, rows), pl.ds(start, cells), :]
            left = left.reshape(rows * cells, 3 * width)
            acc[...] += jnp.dot(
                left, w_vmem[t, :, j * width:(j + 1) * width],
                preferred_element_type=jnp.float32,
            )
            return carry

        lax.fori_loop(0, 9, tap_plane, 0)
        share = acc[...].astype(jnp.bfloat16).reshape(rows, cells, width)
        sbuf[j] = share
        target = c * per_col + j

        @pl.when(target != r)
        def _():
            part_copy(j).start()

        @pl.when(target == r)
        def _():
            pbuf[r] = share

    for row in range(rows):
        @pl.when(row != r)
        def _():
            remote(act_ref, act_all.at[row], act_send.at[row], act_recv.at[row], row=row).wait_recv()

    def pipe_copy(p):
        return remote(gout.at[p], gin.at[p], pipe_send.at[p], gin_recv.at[p], pipe=s - 1)

    def out_copy(p):
        return remote(gout.at[p], sg.at[slot], out_send.at[p], out_recv.at[slot], row=p)

    @pl.when(is_home)
    def _():
        for row in range(rows):
            @pl.when(row != r)
            def _():
                remote(
                    pbuf.at[row], pbuf.at[row], part_send.at[0], part_recv.at[row], row=row
                ).wait_recv()
        for p in range(rows):
            back = pbuf[0, p].astype(jnp.float32)
            for row in range(1, rows):
                back = back + pbuf[row, p].astype(jnp.float32)
            gate = act_all[p, slot] > 0
            fresh = gin[p].astype(jnp.float32) + jnp.where(gate, back, jnp.zeros_like(back))
            gout[p] = fresh.astype(jnp.bfloat16)

            @pl.when(s > 0)
            def _():
                pipe_copy(p).start()

            @pl.when(p != r)
            def _():
                out_copy(p).start()

            @pl.when(p == r)
            def _():
                sg[slot] = gout[p]

    gin_out[...] = gin[...]
    act_out[...] = act_all[...]
    for j in range(per_col):
        @pl.when(c * per_col + j != r)
        def _():
            remote(
                gout.at[0], sg.at[j], out_send.at[0], out_recv.at[j], row=c * per_col + j
            ).wait_recv()
    sg_out[...] = sg[...]

    for j in range(per_col):
        for q in range(cols):
            @pl.when(top_is_far(j, q))
            def _():
                top_copy(j, q).wait_send()

        @pl.when(c * per_col + j != r)
        def _():
            part_copy(j).wait_send()
    for row in range(rows):
        @pl.when(row != r)
        def _():
            act_copy(row).wait_send()
    for p in range(rows):
        for q in range(cols):
            @pl.when(forwards & (q != c))
            def _():
                fwd_copy(p, q).wait_send()

        @pl.when(is_home & (s > 0))
        def _():
            pipe_copy(p).wait_send()

        @pl.when(is_home & (p != r))
        def _():
            out_copy(p).wait_send()


def weight_kernel(scale, gin_ref, act_ref, out_ref, left, field):
    rows, cells, width = gin_ref.shape
    per_col = act_ref.shape[1]

    @pl.when(pl.program_id(0) == 0)
    def _():
        field[...] = jnp.zeros_like(field)
        for p in range(rows):
            left[:, p * cells:(p + 1) * cells] = jnp.transpose(gin_ref[p])
            for j in range(per_col):
                part = jnp.maximum(act_ref[p, j], jnp.zeros_like(act_ref[p, j]))
                for k in range(3):
                    field[k, p + 1, SZ:SZ + cells, j * width:(j + 1) * width] = moved_rows(
                        part, 1 - k
                    )

    t = pl.program_id(0)
    start = pl.multiple_of((t % 3) * SZ, SZ)
    for k in range(3):
        right = field[k, pl.ds(t // 3, rows), pl.ds(start, cells), :]
        right = right.reshape(rows * cells, per_col * width)
        total = jnp.dot(left[...], right, preferred_element_type=jnp.float32)
        out_ref[k] = (total * scale).astype(jnp.bfloat16)


def local(acts, weights, grad_top):
    sections, rows, cols = (lax.axis_size(name) for name in ("pipe", "row", "col"))
    taps, width, depth = weights.shape[1:]
    cells = acts.shape[4]
    per_col = depth // width
    scale = 1.0 / math.sqrt(acts.shape[1] * rows * acts.shape[3] * cells)

    def cells_first(field):
        return jnp.transpose(field.reshape(per_col, width, cells), (0, 2, 1))

    act = cells_first(acts[0, 0])
    top = cells_first(grad_top[0])
    kernel = weights.reshape(taps // 3, 3 * width, depth)
    bf16 = jnp.bfloat16
    vmem = pl.BlockSpec(memory_space=pltpu.VMEM)
    dma = pltpu.SemaphoreType.DMA
    sg, gin, act_all = pl.pallas_call(
        functools.partial(chain_kernel, sections, rows, cols, per_col),
        out_shape=(
            jax.ShapeDtypeStruct((per_col, cells, width), bf16),
            jax.ShapeDtypeStruct((rows, cells, width), bf16),
            jax.ShapeDtypeStruct((rows, per_col, cells, width), bf16),
        ),
        in_specs=[pl.BlockSpec(memory_space=pl.ANY), vmem, vmem],
        out_specs=(vmem, vmem, vmem),
        scratch_shapes=[
            pltpu.VMEM((taps // 3, 3 * width, depth), bf16),
            pltpu.VMEM((rows, cells, width), bf16),
            pltpu.VMEM((rows + 2, cells + 2 * SZ, 3 * width), bf16),
            pltpu.VMEM((rows * cells, width), jnp.float32),
            pltpu.VMEM((per_col, rows, cells, width), bf16),
            pltpu.VMEM((rows, rows, cells, width), bf16),
            pltpu.VMEM((rows, cells, width), bf16),
            pltpu.VMEM((rows, per_col, cells, width), bf16),
            pltpu.VMEM((per_col, cells, width), bf16),
            dma,
            dma((per_col * cols,)),
            dma((rows,)),
            dma((rows, cols)),
            dma((rows,)),
            dma((rows,)),
            dma((per_col,)),
            dma((rows,)),
            dma((rows,)),
            dma((rows,)),
            dma((per_col,)),
        ],
        compiler_params=pltpu.CompilerParams(
            collective_id=0, has_side_effects=True, vmem_limit_bytes=48 * 2**20
        ),
        name="chain",
    )(kernel, act, top)

    weight_grads = pl.pallas_call(
        functools.partial(weight_kernel, scale),
        out_shape=jax.ShapeDtypeStruct((taps, width, depth), bf16),
        grid=(taps // 3,),
        in_specs=[
            pl.BlockSpec((rows, cells, width), lambda t: (0, 0, 0)),
            pl.BlockSpec((rows, per_col, cells, width), lambda t: (0, 0, 0, 0)),
        ],
        out_specs=pl.BlockSpec((3, width, depth), lambda t: (t, 0, 0)),
        scratch_shapes=[
            pltpu.VMEM((width, rows * cells), bf16),
            pltpu.VMEM((3, rows + 2, cells + 2 * SZ, depth), bf16),
        ],
        compiler_params=pltpu.CompilerParams(vmem_limit_bytes=48 * 2**20),
        name="weight",
    )(gin, act_all)
    section_grads = jnp.transpose(sg, (0, 2, 1)).reshape(depth, 1, cells)
    return (section_grads[None, None], weight_grads[None])


def solution(mesh):
    return jax.shard_map(
        local,
        mesh=mesh,
        in_specs=(
            P("pipe", None, "col", "row", None),
            P("pipe", None, "row", "col"),
            P(None, "col", "row", None),
        ),
        out_specs=(P("pipe", None, "col", "row", None), P("pipe", None, "row", "col")),
        check_vma=False,
    )
```

profile of v0, /device:TPU:0, one launch (start us, length us, event | category | flops | bytes accessed | tf_op | source)
XLA Modules:
  0.0 115.5 jit_solution(2961593386629745708)
XLA Ops:
  0.6 1.0 copy.5
  1.6 1.0 copy.6
  2.7 104.3 %chain.1 = (bf16[2,128,256]{2,1,0:T(8,128)(2,1)S(1)}, bf16[4,128,256]{2,1,0:T(8,128)(2,1)S(1)}, bf16[4,2,128,256]{3,2,1,0:T(8,128)(2,1)S(1)}) custom-call(bf16[9,768,512]{2,1,0:T(8,128)(2,1)} %bitcast.11, bf16[2,128,256]{2,1,0:T(8,128)(2,1)S(1)} %bitcast.8, bf16[2,128,256]{2,1,0:T(8,128)(2,1)S(1)} %bitcast.9), custom_call_target="tpu_custom_call" | custom-call | tf_op jit(solution)/shard_map/chain/pallas_call | solution.py:259
  106.9 0.8 copy.7
  107.7 7.8 %weight.1 = bf16[27,256,512]{2,1,0:T(8,128)(2,1)} custom-call(bf16[4,128,256]{2,1,0:T(8,128)(2,1)S(1)} %get-tuple-element.6.gin_ref, bf16[4,2,128,256]{3,2,1,0:T(8,128)(2,1)S(1)} %get-tuple-element.7.act_ref), custom_call_target="tpu_custom_call" | custom-call | tf_op jit(solution)/shard_map/weight/pallas_call | solution.py:296
where the time goes:
time: 116 us
  Pallas kernels  112 us (97%)
  local copies, waits for them, and re-layouts  2.77 us (2%)
    pallas_call x1, Pallas kernels, local(): pl.pallas_call(functools.partial(chain_kernel, sections, rows, cols, per_...  104 us
    pallas_call x1, Pallas kernels, local(): pl.pallas_call(functools.partial(weight_kernel, scale), out_shape=jax.Sha...  7.81 us

commit v1 on v0

v1 whole, which is shorter than its diff:
```python
import functools
import math

import jax
import jax.numpy as jnp
from jax import lax
from jax.experimental import pallas as pl
from jax.experimental.pallas import tpu as pltpu
from jax.sharding import PartitionSpec as P

SZ = 16
MESH = pl.DeviceIdType.MESH


def moved_rows(block, shift):
    if shift == 0:
        return block
    wide = block.astype(jnp.float32)
    rows = wide.shape[0]
    rolled = pltpu.roll(wide, shift % rows, axis=0)
    column = lax.broadcasted_iota(jnp.int32, wide.shape, 0) % SZ
    inside = (column - shift >= 0) & (column - shift < SZ)
    return jnp.where(inside, rolled, jnp.zeros_like(rolled)).astype(block.dtype)


def chain_kernel(
    sections, rows, cols, per_col, scale,
    w_hbm, act_in, top_in,
    sg_out, wg_out,
    w_vmem, act_ref, top_ref, gin, gbuf, acc, sbuf, pbuf, gout, act_all, sg, left, field,
    w_sem, top_send, gin_recv, fwd_send, act_send, act_recv,
    part_send, part_recv, pipe_send, out_send, out_recv,
):
    s, r, c = lax.axis_index("pipe"), lax.axis_index("row"), lax.axis_index("col")
    home = r // per_col
    slot = r % per_col
    cells, width = act_ref.shape[1], act_ref.shape[2]
    half = acc.shape[0] // cells
    halves = rows // half
    is_home = c == home
    is_top = s == sections - 1
    is_last = s == 0

    def remote(src, dst, send, recv, **where):
        return pltpu.make_async_remote_copy(
            src_ref=src, dst_ref=dst, send_sem=send, recv_sem=recv,
            device_id=where, device_id_type=MESH,
        )

    w_copy = pltpu.make_async_copy(w_hbm, w_vmem, w_sem)
    w_copy.start()

    barrier = pltpu.get_barrier_semaphore()
    for step in range(1, rows * cols):
        other = lax.rem(r * cols + c + step, rows * cols)
        pl.semaphore_signal(
            barrier, inc=1, device_id={"row": other // cols, "col": other % cols},
            device_id_type=MESH,
        )
    for step in (1, sections - 1):
        pl.semaphore_signal(
            barrier, inc=1, device_id={"pipe": lax.rem(s + step, sections)},
            device_id_type=MESH,
        )
    for j in range(per_col):
        top_ref[j] = jnp.transpose(top_in[j * width:(j + 1) * width])
    for j in range(per_col):
        act_ref[j] = jnp.transpose(act_in[j * width:(j + 1) * width])
    pl.semaphore_wait(barrier, rows * cols + 1)

    def top_copy(j, q):
        return remote(
            top_ref.at[j], gin.at[r], top_send.at[j * cols + q], gin_recv.at[r],
            row=c * per_col + j, col=q,
        )

    def top_is_far(j, q):
        return is_top & ~((c * per_col + j == r) & (q == c))

    for j in range(per_col):
        for q in range(cols):
            @pl.when(top_is_far(j, q))
            def _():
                top_copy(j, q).start()

    @pl.when(is_top & is_home)
    def _():
        gin[r] = top_ref[slot]

    def act_copy(row, j):
        return remote(
            act_ref.at[j], act_all.at[r, j], act_send.at[row, j], act_recv.at[r, j], row=row
        )

    def act_wait(p, j):
        remote(
            act_ref.at[0], act_all.at[p, j], act_send.at[0, 0], act_recv.at[p, j], row=p
        ).wait_recv()

    def send_other_acts():
        for step in range(1, rows):
            row = lax.rem(r + step, rows)
            for j in range(per_col):
                @pl.when(row != c * per_col + j)
                def _():
                    act_copy(row, j).start()

    def build_field():
        for p in range(rows):
            for j in range(per_col):
                part = act_all[p, j]
                part = jnp.maximum(part, jnp.zeros_like(part))
                for k in range(3):
                    field[k, p + 1, SZ:SZ + cells, j * width:(j + 1) * width] = moved_rows(
                        part, 1 - k
                    )

    for j in range(per_col):
        @pl.when(r != c * per_col + j)
        def _():
            act_copy(c * per_col + j, j).start()
    act_all[r] = act_ref[...]
    gbuf[...] = jnp.zeros_like(gbuf)
    field[...] = jnp.zeros_like(field)

    @pl.when(~is_top)
    def _():
        send_other_acts()
        for p in range(rows):
            @pl.when(p != r)
            def _():
                for j in range(per_col):
                    act_wait(p, j)
        build_field()

    def fwd_copy(p, q):
        return remote(gin.at[p], gin.at[p], fwd_send.at[p, q], gin_recv.at[p], col=q)

    forwards = is_home & (s < sections - 1)
    w_copy.wait()
    for p in range(rows):
        @pl.when(~(is_top & is_home & (p == r)))
        def _():
            remote(gin.at[p], gin.at[p], fwd_send.at[p, 0], gin_recv.at[p], col=c).wait_recv()
        for q in range(cols):
            @pl.when(forwards & (q != c))
            def _():
                fwd_copy(p, q).start()
        for k in range(3):
            gbuf[p + 1, SZ:SZ + cells, k * width:(k + 1) * width] = moved_rows(gin[p], k - 1)

    def part_copy(j, h):
        return remote(
            sbuf.at[j, pl.ds(h * half, half)], pbuf.at[r, pl.ds(h * half, half)],
            part_send.at[j, h], part_recv.at[r, h], row=c * per_col + j,
        )

    for h in range(halves):
        for j in range(per_col):
            acc[...] = jnp.zeros_like(acc)

            def tap_plane(t, carry):
                start = pl.multiple_of((2 - t % 3) * SZ, SZ)
                rhs = w_vmem[t, :, j * width:(j + 1) * width]
                lhs = gbuf[pl.ds(2 - t // 3 + h * half, half), pl.ds(start, cells), :]
                acc[...] += jnp.dot(
                    lhs.reshape(half * cells, 3 * width), rhs,
                    preferred_element_type=jnp.float32,
                )
                return carry

            lax.fori_loop(0, 9, tap_plane, 0)
            share = acc[...].astype(jnp.bfloat16).reshape(half, cells, width)
            sbuf[j, h * half:(h + 1) * half] = share
            target = c * per_col + j

            @pl.when(target != r)
            def _():
                part_copy(j, h).start()

            @pl.when(target == r)
            def _():
                pbuf[r, h * half:(h + 1) * half] = share

    def weight_grads():
        for p in range(rows):
            left[:, p * cells:(p + 1) * cells] = jnp.transpose(gin[p])

        def tap_plane(t, carry):
            start = pl.multiple_of((t % 3) * SZ, SZ)
            for k in range(3):
                right = field[k, pl.ds(t // 3, rows), pl.ds(start, cells), :]
                right = right.reshape(rows * cells, per_col * width)
                total = jnp.dot(left[...], right, preferred_element_type=jnp.float32)
                wg_out[3 * t + k] = (total * scale).astype(jnp.bfloat16)
            return carry

        lax.fori_loop(0, 9, tap_plane, 0)

    @pl.when(is_last)
    def _():
        weight_grads()

    @pl.when(is_top)
    def _():
        send_other_acts()

    def pipe_copy(p):
        return remote(gout.at[p], gin.at[p], pipe_send.at[p], gin_recv.at[p], pipe=s - 1)

    def out_copy(p):
        return remote(gout.at[p], sg.at[slot], out_send.at[p], out_recv.at[slot], row=p)

    @pl.when(is_home)
    def _():
        for p in range(rows):
            @pl.when(is_top & (p != r))
            def _():
                act_wait(p, slot)
        for h in range(halves):
            for row in range(rows):
                @pl.when(row != r)
                def _():
                    remote(
                        pbuf.at[row, pl.ds(h * half, half)], pbuf.at[row, pl.ds(h * half, half)],
                        part_send.at[0, 0], part_recv.at[row, h], row=row,
                    ).wait_recv()
            for p in range(h * half, (h + 1) * half):
                back = pbuf[0, p].astype(jnp.float32)
                for row in range(1, rows):
                    back = back + pbuf[row, p].astype(jnp.float32)
                gate = act_all[p, slot] > 0
                fresh = gin[p].astype(jnp.float32) + jnp.where(gate, back, jnp.zeros_like(back))
                gout[p] = fresh.astype(jnp.bfloat16)

                @pl.when(s > 0)
                def _():
                    pipe_copy(p).start()
        for p in range(rows):
            @pl.when(p != r)
            def _():
                out_copy(p).start()
        sg[slot] = gout[r]

    @pl.when(is_top)
    def _():
        for p in range(rows):
            for j in range(per_col):
                @pl.when((p != r) & ~(is_home & (j == slot)))
                def _():
                    act_wait(p, j)
        build_field()

    @pl.when(~is_last)
    def _():
        weight_grads()

    for j in range(per_col):
        @pl.when(c * per_col + j != r)
        def _():
            remote(
                gout.at[0], sg.at[j], out_send.at[0], out_recv.at[j], row=c * per_col + j
            ).wait_recv()
        sg_out[j * width:(j + 1) * width] = jnp.transpose(sg[j])

    for j in range(per_col):
        for q in range(cols):
            @pl.when(top_is_far(j, q))
            def _():
                top_copy(j, q).wait_send()
        for h in range(halves):
            @pl.when(c * per_col + j != r)
            def _():
                part_copy(j, h).wait_send()
    for row in range(rows):
        @pl.when(row != r)
        def _():
            for j in range(per_col):
                act_copy(row, j).wait_send()
    for p in range(rows):
        for q in range(cols):
            @pl.when(forwards & (q != c))
            def _():
                fwd_copy(p, q).wait_send()

        @pl.when(is_home & (s > 0))
        def _():
            pipe_copy(p).wait_send()

        @pl.when(is_home & (p != r))
        def _():
            out_copy(p).wait_send()


def local(acts, weights, grad_top):
    sections, rows, cols = (lax.axis_size(name) for name in ("pipe", "row", "col"))
    taps, width, depth = weights.shape[1:]
    cells = acts.shape[4]
    per_col = depth // width
    half = rows // 2
    scale = 1.0 / math.sqrt(acts.shape[1] * rows * acts.shape[3] * cells)
    kernel = weights.reshape(taps // 3, 3 * width, depth)
    bf16 = jnp.bfloat16
    vmem = pl.BlockSpec(memory_space=pltpu.VMEM)
    dma = pltpu.SemaphoreType.DMA
    section_grads, weight_grads = pl.pallas_call(
        functools.partial(chain_kernel, sections, rows, cols, per_col, scale),
        out_shape=(
            jax.ShapeDtypeStruct((depth, cells), bf16),
            jax.ShapeDtypeStruct((taps, width, depth), bf16),
        ),
        in_specs=[pl.BlockSpec(memory_space=pltpu.HBM), vmem, vmem],
        out_specs=(vmem, vmem),
        scratch_shapes=[
            pltpu.VMEM((taps // 3, 3 * width, depth), bf16),
            pltpu.VMEM((per_col, cells, width), bf16),
            pltpu.VMEM((per_col, cells, width), bf16),
            pltpu.VMEM((rows, cells, width), bf16),
            pltpu.VMEM((rows + 2, cells + 2 * SZ, 3 * width), bf16),
            pltpu.VMEM((half * cells, width), jnp.float32),
            pltpu.VMEM((per_col, rows, cells, width), bf16),
            pltpu.VMEM((rows, rows, cells, width), bf16),
            pltpu.VMEM((rows, cells, width), bf16),
            pltpu.VMEM((rows, per_col, cells, width), bf16),
            pltpu.VMEM((per_col, cells, width), bf16),
            pltpu.VMEM((width, rows * cells), bf16),
            pltpu.VMEM((3, rows + 2, cells + 2 * SZ, depth), bf16),
            dma,
            dma((per_col * cols,)),
            dma((rows,)),
            dma((rows, cols)),
            dma((rows, per_col)),
            dma((rows, per_col)),
            dma((per_col, 2)),
            dma((rows, 2)),
            dma((rows,)),
            dma((rows,)),
            dma((per_col,)),
        ],
        compiler_params=pltpu.CompilerParams(
            collective_id=0, has_side_effects=True, vmem_limit_bytes=36 * 2**20
        ),
        name="chain",
    )(kernel, acts.reshape(depth, cells), grad_top.reshape(depth, cells))
    return (section_grads.reshape(acts.shape), weight_grads[None])


def solution(mesh):
    return jax.shard_map(
        local,
        mesh=mesh,
        in_specs=(
            P("pipe", None, "col", "row", None),
            P("pipe", None, "row", "col"),
            P(None, "col", "row", None),
        ),
        out_specs=(P("pipe", None, "col", "row", None), P("pipe", None, "row", "col")),
        check_vma=False,
    )
```

time: 116 us -> 112 us (0.966)
  Pallas kernels: 112 us -> 102 us
  local copies, waits for them, and re-layouts: 2.77 us -> 8.43 us
    unnamed x0 -> x8, local copies, waits for them, and re-layouts: none -> 8.43 us
    pallas_call x1 -> x0, Pallas kernels: 7.81 us -> none  [local(): pl.pallas_call(functools.partial(weight_kernel, scale), out_shape=jax.Sha...]
    another operation x2 -> x0, local copies, waits for them, and re-layouts: 2.01 us -> none  [cells_first(): return jnp.transpose(field.reshape(per_col, width, cells), (0, 2, 1))]
    pallas_call x1, Pallas kernels: 104 us -> 102 us  [local(): pl.pallas_call(functools.partial(chain_kernel, sections, rows, cols, per_...]
where the time goes in v1:
time: 112 us
  Pallas kernels  102 us (91%)
  local copies, waits for them, and re-layouts  8.43 us (8%)
    pallas_call x1, Pallas kernels, local(): pl.pallas_call(functools.partial(chain_kernel, sections, rows, cols, per_...  102 us
    unnamed x8, local copies, waits for them, and re-layouts  8.43 us

profile of v1, /device:TPU:0, one launch (start us, length us, event | category | flops | bytes accessed | tf_op | source)
XLA Modules:
  0.0 111.6 jit_solution(9454590135261104708)
XLA Ops:
  0.6 0.0 copy-start
  0.6 3.0 %copy-done = bf16[1,27,256,512]{3,2,1,0:T(8,128)(2,1)S(1)} copy-done((bf16[1,27,256,512]{3,2,1,0:T(8,128)(2,1)S(1)}, bf16[1,27,256,512]{3,2,1,0:T(8,128)(2,1)}, u32[]{:S(2)}) %copy-start) | copy-done | bytes 7077912
  3.6 0.0 copy-start.1
  3.6 0.9 copy-done.1
  4.5 0.0 copy-start.2
  4.5 0.9 copy-done.2
  5.4 102.5 %chain.1 = (bf16[512,128]{1,0:T(8,128)(2,1)S(1)}, bf16[27,256,512]{2,1,0:T(8,128)(2,1)S(1)}) custom-call(bf16[9,768,512]{2,1,0:T(8,128)(2,1)S(1)} %bitcast.5, bf16[512,128]{1,0:T(8,128)(2,1)S(1)} %bitcast.7, bf16[512,128]{1,0:T(8,128)(2,1)S(1)} %bitcast.8), custom_call_target="tpu_custom_call" | custom-call | tf_op jit(solution)/shard_map/chain/pallas_call | solution.py:306
  108.0 0.7 copy.7
  108.6 3.0 %copy.8 = bf16[1,27,256,512]{3,2,1,0:T(8,128)(2,1)} copy(bf16[1,27,256,512]{3,2,1,0:T(8,128)(2,1)S(1)} %bitcast.6) | data formatting | bytes 14155776
Async XLA Ops:
  0.6 3.0 %copy-start = (bf16[1,27,256,512]{3,2,1,0:T(8,128)(2,1)S(1)}, bf16[1,27,256,512]{3,2,1,0:T(8,128)(2,1)}, u32[]{:S(2)}) copy-start(bf16[1,27,256,512]{3,2,1,0:T(8,128)(2,1)} %param.4) | copy-start | bytes 21233668
  3.6 0.9 copy-start.1
  4.5 0.9 copy-start.2

commit v2 on v1

--- a/solution.py
+++ b/solution.py
@@ -51,37 +51,28 @@
     w_copy.start()
 
     barrier = pltpu.get_barrier_semaphore()
-    for step in range(1, rows * cols):
-        other = lax.rem(r * cols + c + step, rows * cols)
+    partners = [("row", r, step, rows) for step in range(1, rows)]
+    partners += [("col", c, step, cols) for step in range(1, cols)]
+    partners += [("pipe", s, step, sections) for step in (1, sections - 1)]
+    for axis, own, step, size in partners:
         pl.semaphore_signal(
-            barrier, inc=1, device_id={"row": other // cols, "col": other % cols},
-            device_id_type=MESH,
-        )
-    for step in (1, sections - 1):
-        pl.semaphore_signal(
-            barrier, inc=1, device_id={"pipe": lax.rem(s + step, sections)},
-            device_id_type=MESH,
+            barrier, inc=1, device_id={axis: lax.rem(own + step, size)}, device_id_type=MESH
         )
     for j in range(per_col):
         top_ref[j] = jnp.transpose(top_in[j * width:(j + 1) * width])
+    pl.semaphore_wait(barrier, len(partners))
+
+    def top_copy(j):
+        return remote(
+            top_ref.at[j], gin.at[r], top_send.at[j], gin_recv.at[r], row=c * per_col + j
+        )
+
+    for j in range(per_col):
+        @pl.when(is_top & (c * per_col + j != r))
+        def _():
+            top_copy(j).start()
     for j in range(per_col):
         act_ref[j] = jnp.transpose(act_in[j * width:(j + 1) * width])
-    pl.semaphore_wait(barrier, rows * cols + 1)
-
-    def top_copy(j, q):
-        return remote(
-            top_ref.at[j], gin.at[r], top_send.at[j * cols + q], gin_recv.at[r],
-            row=c * per_col + j, col=q,
-        )
-
-    def top_is_far(j, q):
-        return is_top & ~((c * per_col + j == r) & (q == c))
-
-    for j in range(per_col):
-        for q in range(cols):
-            @pl.when(top_is_far(j, q))
-            def _():
-                top_copy(j, q).start()
 
     @pl.when(is_top & is_home)
     def _():
@@ -106,6 +97,7 @@
                     act_copy(row, j).start()
 
     def build_field():
+        field[...] = jnp.zeros_like(field)
         for p in range(rows):
             for j in range(per_col):
                 part = act_all[p, j]
@@ -121,7 +113,6 @@
             act_copy(c * per_col + j, j).start()
     act_all[r] = act_ref[...]
     gbuf[...] = jnp.zeros_like(gbuf)
-    field[...] = jnp.zeros_like(field)
 
     @pl.when(~is_top)
     def _():
@@ -136,26 +127,43 @@
     def fwd_copy(p, q):
         return remote(gin.at[p], gin.at[p], fwd_send.at[p, q], gin_recv.at[p], col=q)
 
-    forwards = is_home & (s < sections - 1)
-    w_copy.wait()
-    for p in range(rows):
+    def take_plane(p):
         @pl.when(~(is_top & is_home & (p == r)))
         def _():
             remote(gin.at[p], gin.at[p], fwd_send.at[p, 0], gin_recv.at[p], col=c).wait_recv()
         for q in range(cols):
-            @pl.when(forwards & (q != c))
+            @pl.when(is_home & (q != c))
             def _():
                 fwd_copy(p, q).start()
         for k in range(3):
             gbuf[p + 1, SZ:SZ + cells, k * width:(k + 1) * width] = moved_rows(gin[p], k - 1)
 
-    def part_copy(j, h):
+    def part_copy(j, p):
         return remote(
-            sbuf.at[j, pl.ds(h * half, half)], pbuf.at[r, pl.ds(h * half, half)],
-            part_send.at[j, h], part_recv.at[r, h], row=c * per_col + j,
-        )
-
+            sbuf.at[j, p], pbuf.at[r, p], part_send.at[j, p], part_recv.at[r, p],
+            row=c * per_col + j,
+        )
+
+    def send_shares(j, planes):
+        @pl.when(c * per_col + j != r)
+        def _():
+            for p in planes:
+                part_copy(j, p).start()
+
+        @pl.when(c * per_col + j == r)
+        def _():
+            for p in planes:
+                pbuf[r, p] = sbuf[j, p]
+
+    w_copy.wait()
+    taken = 0
     for h in range(halves):
+        needed = min(rows, (h + 1) * half + 1)
+        for p in range(taken, needed):
+            take_plane(p)
+        taken = needed
+        planes = list(range(h * half, (h + 1) * half))
+        late = planes[-1:] if h == halves - 1 else []
         for j in range(per_col):
             acc[...] = jnp.zeros_like(acc)
 
@@ -172,15 +180,9 @@
             lax.fori_loop(0, 9, tap_plane, 0)
             share = acc[...].astype(jnp.bfloat16).reshape(half, cells, width)
             sbuf[j, h * half:(h + 1) * half] = share
-            target = c * per_col + j
-
-            @pl.when(target != r)
-            def _():
-                part_copy(j, h).start()
-
-            @pl.when(target == r)
-            def _():
-                pbuf[r, h * half:(h + 1) * half] = share
+            send_shares(j, [p for p in planes if p not in late])
+        for j in range(per_col):
+            send_shares(j, late)
 
     def weight_grads():
         for p in range(rows):
@@ -201,10 +203,6 @@
     def _():
         weight_grads()
 
-    @pl.when(is_top)
-    def _():
-        send_other_acts()
-
     def pipe_copy(p):
         return remote(gout.at[p], gin.at[p], pipe_send.at[p], gin_recv.at[p], pipe=s - 1)
 
@@ -217,33 +215,41 @@
             @pl.when(is_top & (p != r))
             def _():
                 act_wait(p, slot)
-        for h in range(halves):
+        for p in range(rows):
             for row in range(rows):
                 @pl.when(row != r)
                 def _():
                     remote(
-                        pbuf.at[row, pl.ds(h * half, half)], pbuf.at[row, pl.ds(h * half, half)],
-                        part_send.at[0, 0], part_recv.at[row, h], row=row,
+                        pbuf.at[row, p], pbuf.at[row, p], part_send.at[0, 0],
+                        part_recv.at[row, p], row=row,
                     ).wait_recv()
-            for p in range(h * half, (h + 1) * half):
-                back = pbuf[0, p].astype(jnp.float32)
-                for row in range(1, rows):
-                    back = back + pbuf[row, p].astype(jnp.float32)
-                gate = act_all[p, slot] > 0
-                fresh = gin[p].astype(jnp.float32) + jnp.where(gate, back, jnp.zeros_like(back))
-                gout[p] = fresh.astype(jnp.bfloat16)
-
-                @pl.when(s > 0)
-                def _():
-                    pipe_copy(p).start()
+            back = pbuf[0, p].astype(jnp.float32)
+            for row in range(1, rows):
+                back = back + pbuf[row, p].astype(jnp.float32)
+            gate = act_all[p, slot] > 0
+            fresh = gin[p].astype(jnp.float32) + jnp.where(gate, back, jnp.zeros_like(back))
+            gout[p] = fresh.astype(jnp.bfloat16)
+
+            @pl.when(s > 0)
+            def _():
+                pipe_copy(p).start()
         for p in range(rows):
             @pl.when(p != r)
             def _():
                 out_copy(p).start()
         sg[slot] = gout[r]
 
+    for j in range(per_col):
+        @pl.when(c * per_col + j != r)
+        def _():
+            remote(
+                gout.at[0], sg.at[j], out_send.at[0], out_recv.at[j], row=c * per_col + j
+            ).wait_recv()
+        sg_out[j * width:(j + 1) * width] = jnp.transpose(sg[j])
+
     @pl.when(is_top)
     def _():
+        send_other_acts()
         for p in range(rows):
             for j in range(per_col):
                 @pl.when((p != r) & ~(is_home & (j == slot)))
@@ -256,22 +262,14 @@
         weight_grads()
 
     for j in range(per_col):
+        @pl.when(is_top & (c * per_col + j != r))
+        def _():
+            top_copy(j).wait_send()
+
         @pl.when(c * per_col + j != r)
         def _():
-            remote(
-                gout.at[0], sg.at[j], out_send.at[0], out_recv.at[j], row=c * per_col + j
-            ).wait_recv()
-        sg_out[j * width:(j + 1) * width] = jnp.transpose(sg[j])
-
-    for j in range(per_col):
-        for q in range(cols):
-            @pl.when(top_is_far(j, q))
-            def _():
-                top_copy(j, q).wait_send()
-        for h in range(halves):
-            @pl.when(c * per_col + j != r)
-            def _():
-                part_copy(j, h).wait_send()
+            for p in range(rows):
+                part_copy(j, p).wait_send()
     for row in range(rows):
         @pl.when(row != r)
         def _():
@@ -279,7 +277,7 @@
                 act_copy(row, j).wait_send()
     for p in range(rows):
         for q in range(cols):
-            @pl.when(forwards & (q != c))
+            @pl.when(is_home & (q != c))
             def _():
                 fwd_copy(p, q).wait_send()
 
@@ -326,19 +324,19 @@
             pltpu.VMEM((width, rows * cells), bf16),
             pltpu.VMEM((3, rows + 2, cells + 2 * SZ, depth), bf16),
             dma,
-            dma((per_col * cols,)),
+            dma((per_col,)),
             dma((rows,)),
             dma((rows, cols)),
             dma((rows, per_col)),
             dma((rows, per_col)),
-            dma((per_col, 2)),
-            dma((rows, 2)),
+            dma((per_col, rows)),
+            dma((rows, rows)),
             dma((rows,)),
             dma((rows,)),
             dma((per_col,)),
         ],
         compiler_params=pltpu.CompilerParams(
-            collective_id=0, has_side_effects=True, vmem_limit_bytes=36 * 2**20
+            collective_id=0, has_side_effects=True, vmem_limit_bytes=44 * 2**20
         ),
         name="chain",
     )(kernel, acts.reshape(depth, cells), grad_top.reshape(depth, cells))

time: 112 us -> 92.9 us (0.83)
  Pallas kernels: 102 us -> 86.7 us
  local copies, waits for them, and re-layouts: 8.43 us -> 5.42 us
    pallas_call x1, Pallas kernels: 102 us -> 86.7 us  [local(): pl.pallas_call(functools.partial(chain_kernel, sections, rows, cols, per_...]
    unnamed x8 -> x6, local copies, waits for them, and re-layouts: 8.43 us -> 5.42 us
where the time goes in v2:
time: 92.9 us; the launch traced here: 92.7 us
  Pallas kernels  86.7 us (93%)
  local copies, waits for them, and re-layouts  5.42 us (6%)
    pallas_call x1, Pallas kernels, local(): pl.pallas_call(functools.partial(chain_kernel, sections, rows, cols, per_...  86.7 us
    unnamed x6, local copies, waits for them, and re-layouts  5.42 us

profile of v2, /device:TPU:0, one launch (start us, length us, event | category | flops | bytes accessed | tf_op | source)
XLA Modules:
  0.0 92.7 jit_solution(13737092851594894152)
XLA Ops:
  0.6 0.0 copy-start
  0.6 0.9 copy-done
  1.5 0.0 copy-start.1
  1.5 0.9 copy-done.1
  2.4 86.7 %chain.1 = (bf16[512,128]{1,0:T(8,128)(2,1)S(1)}, bf16[27,256,512]{2,1,0:T(8,128)(2,1)S(1)}) custom-call(bf16[9,768,512]{2,1,0:T(8,128)(2,1)} %bitcast.9, bf16[512,128]{1,0:T(8,128)(2,1)S(1)} %bitcast.6, bf16[512,128]{1,0:T(8,128)(2,1)S(1)} %bitcast.7), custom_call_target="tpu_custom_call" | custom-call | tf_op jit(solution)/shard_map/chain/pallas_call | solution.py:304
  89.1 0.7 copy.7
  89.8 3.0 %copy.8 = bf16[1,27,256,512]{3,2,1,0:T(8,128)(2,1)} copy(bf16[1,27,256,512]{3,2,1,0:T(8,128)(2,1)S(1)} %bitcast.5) | data formatting | bytes 14155776
Async XLA Ops:
  0.6 0.9 copy-start
  1.5 0.9 copy-start.1

commit v3 on v2

--- a/solution.py
+++ b/solution.py
@@ -177,17 +177,18 @@
                 )
                 return carry
 
-            lax.fori_loop(0, 9, tap_plane, 0)
+            lax.fori_loop(0, 9, tap_plane, 0, unroll=3)
             share = acc[...].astype(jnp.bfloat16).reshape(half, cells, width)
             sbuf[j, h * half:(h + 1) * half] = share
             send_shares(j, [p for p in planes if p not in late])
         for j in range(per_col):
             send_shares(j, late)
 
-    def weight_grads():
+    def turn_grads():
         for p in range(rows):
             left[:, p * cells:(p + 1) * cells] = jnp.transpose(gin[p])
 
+    def weight_grads(first, last):
         def tap_plane(t, carry):
             start = pl.multiple_of((t % 3) * SZ, SZ)
             for k in range(3):
@@ -197,11 +198,12 @@
                 wg_out[3 * t + k] = (total * scale).astype(jnp.bfloat16)
             return carry
 
-        lax.fori_loop(0, 9, tap_plane, 0)
+        lax.fori_loop(first, last, tap_plane, 0)
 
     @pl.when(is_last)
     def _():
-        weight_grads()
+        turn_grads()
+        weight_grads(0, 5)
 
     def pipe_copy(p):
         return remote(gout.at[p], gin.at[p], pipe_send.at[p], gin_recv.at[p], pipe=s - 1)
@@ -239,6 +241,10 @@
                 out_copy(p).start()
         sg[slot] = gout[r]
 
+    @pl.when(is_last)
+    def _():
+        weight_grads(5, 9)
+
     for j in range(per_col):
         @pl.when(c * per_col + j != r)
         def _():
@@ -259,7 +265,8 @@
 
     @pl.when(~is_last)
     def _():
-        weight_grads()
+        turn_grads()
+        weight_grads(0, 9)
 
     for j in range(per_col):
         @pl.when(is_top & (c * per_col + j != r))

time: 92.9 us -> 88.4 us (0.952)
  Pallas kernels: 86.7 us -> 82.2 us
    pallas_call x1, Pallas kernels: 86.7 us -> 82.2 us  [local(): pl.pallas_call(functools.partial(chain_kernel, sections, rows, cols, per_...]
where the time goes in v3:
time: 88.4 us; the launch traced here: 88.3 us
  Pallas kernels  82.2 us (93%)
  local copies, waits for them, and re-layouts  5.42 us (6%)
    pallas_call x1, Pallas kernels, local(): pl.pallas_call(functools.partial(chain_kernel, sections, rows, cols, per_...  82.2 us
    unnamed x6, local copies, waits for them, and re-layouts  5.42 us

profile of v3, /device:TPU:0, one launch (start us, length us, event | category | flops | bytes accessed | tf_op | source)
XLA Modules:
  0.0 88.3 jit_solution(3414057227292926203)
XLA Ops:
  0.6 0.0 copy-start
  0.6 0.9 %copy-done = bf16[1,1,512,1,128]{4,2,3,1,0:T(8,128)(2,1)S(1)} copy-done((bf16[1,1,512,1,128]{4,2,3,1,0:T(8,128)(2,1)S(1)}, bf16[1,1,512,1,128]{4,2,3,1,0:T(8,128)(2,1)}, u32[]{:S(2)}) %copy-start) | copy-done | bytes 131096
  1.5 0.0 copy-start.1
  1.5 0.9 %copy-done.1 = bf16[1,512,1,128]{3,1,2,0:T(8,128)(2,1)S(1)} copy-done((bf16[1,512,1,128]{3,1,2,0:T(8,128)(2,1)S(1)}, bf16[1,512,1,128]{3,1,2,0:T(8,128)(2,1)}, u32[]{:S(2)}) %copy-start.1) | copy-done | bytes 131096
  2.4 82.2 %chain.1 = (bf16[512,128]{1,0:T(8,128)(2,1)S(1)}, bf16[27,256,512]{2,1,0:T(8,128)(2,1)S(1)}) custom-call(bf16[9,768,512]{2,1,0:T(8,128)(2,1)} %bitcast.9, bf16[512,128]{1,0:T(8,128)(2,1)S(1)} %bitcast.6, bf16[512,128]{1,0:T(8,128)(2,1)S(1)} %bitcast.7), custom_call_target="tpu_custom_call" | custom-call | tf_op jit(solution)/shard_map/chain/pallas_call | solution.py:311
  84.6 0.7 copy.7
  85.3 3.0 %copy.8 = bf16[1,27,256,512]{3,2,1,0:T(8,128)(2,1)} copy(bf16[1,27,256,512]{3,2,1,0:T(8,128)(2,1)S(1)} %bitcast.5) | data formatting | bytes 14155776
Async XLA Ops:
  0.6 0.9 %copy-start = (bf16[1,1,512,1,128]{4,2,3,1,0:T(8,128)(2,1)S(1)}, bf16[1,1,512,1,128]{4,2,3,1,0:T(8,128)(2,1)}, u32[]{:S(2)}) copy-start(bf16[1,1,512,1,128]{4,2,3,1,0:T(8,128)(2,1)} %param.3) | copy-start | bytes 393220
  1.5 0.9 %copy-start.1 = (bf16[1,512,1,128]{3,1,2,0:T(8,128)(2,1)S(1)}, bf16[1,512,1,128]{3,1,2,0:T(8,128)(2,1)}, u32[]{:S(2)}) copy-start(bf16[1,512,1,128]{3,1,2,0:T(8,128)(2,1)} %param.5) | copy-start | bytes 393220
